TPU v7x, 512 devices: a whole 4x4x16 slice. The times are simulated.
512 devices in a mesh: dp: 32 (over z, core), mp: 16 (over x, y).
Axes of the slice: x: 4, y: 4, z: 16, core: 2. Of those that a mesh axis runs over, the one named last changes fastest.
Arguments:
- stream_in: bfloat16 [2048, 2048], P('dp', 'mp'), parts along dimension 0, may hold values from -24 to 24
- norm_gain: bfloat16 [2048], P('mp'), may hold values from 0.5 to 2
- gate_vals: bfloat16 [1024, 8192], P(None, 'mp'), may hold values from -0.1875 to 0.1875
- gate_mask: int32 [64, 8192], P(None, 'mp'), may hold values from 0 to 1679615
- up_vals: bfloat16 [1024, 8192], P(None, 'mp'), may hold values from -0.1875 to 0.1875
- up_mask: int32 [64, 8192], P(None, 'mp'), may hold values from 0 to 1679615
- down_vals: bfloat16 [4096, 2048], P('mp'), may hold values from -0.125 to 0.125
- down_mask: int32 [256, 2048], P('mp'), may hold values from 0 to 1679615
- final_gain: bfloat16 [2048], P('mp'), may hold values from 0.5 to 2
Outputs:
- stream_out: bfloat16 [2048, 2048], P('dp', 'mp'), parts along dimension 0
- final_normed: bfloat16 [2048, 2048], P('dp', 'mp'), parts along dimension 0
There are 32 independent parts, one for each index of `dp`. A program takes and returns all parts, laid end to end along the dimension named above; an argument that names none is the same for every part. Nothing has to cross between parts.
Inputs may be any that keep to these rules, and one draw needn't show every extreme that they name: `gate_mask`: eight base-6 digits per entry, as the steps decode them. `up_mask`: eight base-6 digits per entry, as the steps decode them. `down_mask`: eight base-6 digits per entry, as the steps decode them.
All inputs are finite; a program needn't handle non-finite values.
Results may differ from a plain program's by a relative error of at most 0.017.
Values may be sent and summed in bfloat16 or wider, within the bound.
A program may use at most 64 MiB of HBM per device.

v0:
```python
import jax
import jax.numpy as jnp
from jax import lax
from jax.sharding import PartitionSpec as P

epsilon = 1e-05


def in_order(parts, dim):
    parts = jnp.moveaxis(parts, 0, dim)
    lengths = parts.shape
    return parts.reshape(*lengths[:dim], lengths[dim] * lengths[dim + 1], *lengths[dim + 2 :])


def from_everyone(array, axis):
    size = lax.axis_size(axis)
    return lax.all_to_all(
        jnp.broadcast_to(array[None], (size, *array.shape)), axis, 0, 0, tiled=True
    )


def gathered_copies(array, axis, dim):
    return in_order(from_everyone(array, axis), dim)


def cut_along(array, dim, size):
    lengths = array.shape
    parts = array.reshape(*lengths[:dim], size, lengths[dim] // size, *lengths[dim + 1 :])
    return jnp.moveaxis(parts, dim, 0)


def sum_at_owner(array, axis, dim):
    size = lax.axis_size(axis)
    parts = lax.all_to_all(cut_along(array, dim, size), axis, 0, 0, tiled=True)
    return jnp.sum(parts.astype(jnp.float32), axis=0)


def taken_together(array, axis):
    return from_everyone(array, axis).sum(axis=0)


def expand(values, packed):
    powers = jnp.array([6**digit_index for digit_index in range(8)], jnp.int32)
    digits = (packed[:, None, :] // powers[None, :, None] % 6).reshape(
        packed.shape[0] * 8, packed.shape[1]
    )
    paired = values.reshape(digits.shape[0], 2, values.shape[1])
    first_val = paired[:, 0, :]
    second_val = paired[:, 1, :]
    zero_val = jnp.zeros((), values.dtype)
    row_zero = jnp.where(digits < 3, first_val, zero_val)
    row_one = jnp.where(
        digits == 0, second_val, jnp.where((digits == 3) | (digits == 4), first_val, zero_val)
    )
    row_two = jnp.where(
        digits == 5, first_val, jnp.where((digits == 1) | (digits == 3), second_val, zero_val)
    )
    row_three = jnp.where((digits == 2) | (digits >= 4), second_val, zero_val)
    dense = jnp.stack([row_zero, row_one, row_two, row_three], axis=1)
    return dense.reshape(digits.shape[0] * 4, values.shape[1])


def shards(
    stream_in, norm_gain, gate_vals, gate_mask, up_vals, up_mask, down_vals, down_mask, final_gain
):
    width_local = stream_in.shape[1]
    width_full = width_local * lax.axis_size("mp")
    stream_f = stream_in.astype(jnp.float32)
    gate_dense = expand(gate_vals, gate_mask)
    up_dense = expand(up_vals, up_mask)
    gathered, gain_full = (gathered_copies(stream_in, "mp", 1), gathered_copies(norm_gain, "mp", 0))
    gathered_f = gathered.astype(jnp.float32)
    mean_sq = jnp.mean(gathered_f * gathered_f, axis=1, keepdims=True)
    normed = (gathered_f * lax.rsqrt(mean_sq + epsilon) * gain_full.astype(jnp.float32)).astype(
        jnp.bfloat16
    )
    gate_part = jnp.dot(normed, gate_dense, preferred_element_type=jnp.float32)
    up_part = jnp.dot(normed, up_dense, preferred_element_type=jnp.float32)
    hidden = (jax.nn.silu(gate_part) * up_part).astype(jnp.bfloat16)
    down_dense = expand(down_vals, down_mask)
    partial_term = jnp.dot(hidden, down_dense, preferred_element_type=jnp.float32)
    summed = sum_at_owner(partial_term.astype(jnp.bfloat16), "mp", 1)
    stream_out = (stream_f + summed).astype(jnp.bfloat16)
    out_f = stream_out.astype(jnp.float32)
    final_total = taken_together(jnp.sum(out_f * out_f, axis=1), "mp")
    final_scale = lax.rsqrt(final_total / width_full + epsilon)
    final_normed = (out_f * final_scale[:, None] * final_gain.astype(jnp.float32)).astype(
        jnp.bfloat16
    )
    return (stream_out, final_normed)


def solution(mesh):
    placed = (
        P("dp", "mp"),
        P("mp"),
        P(None, "mp"),
        P(None, "mp"),
        P(None, "mp"),
        P(None, "mp"),
        P("mp", None),
        P("mp", None),
        P("mp"),
    )
    return jax.shard_map(
        shards,
        mesh=mesh,
        in_specs=placed,
        out_specs=(P("dp", "mp"), P("dp", "mp")),
        check_vma=False,
    )
```

profile of v0, /device:TPU:2, one launch (start us, length us, event | category | flops | bytes accessed | tf_op | source)
XLA Modules:
  0.0 122.7 jit_solution(17541034352392915842)
XLA Ops:
  0.6 1.3 %broadcast_in_dim.55 = bf16[16,1,128]{2,1,0:T(2,128)(2,1)} broadcast(bf16[128]{0:T(256)(128)(2,1)} %param.15), dimensions={2} | broadcast | bytes 4352 | tf_op jit(solution)/shard_map/broadcast_in_dim | solution.py:18
  1.9 9.2 %all-to-all-start.1 = ((bf16[16,1,128]{2,1,0:T(2,128)(2,1)}), bf16[16,1,128]{2,1,0:T(2,128)(2,1)S(1)}, u32[]{:S(2)}, u32[]{:S(2)}) async-start(bf16[16,1,128]{2,1,0:T(2,128)(2,1)} %broadcast_in_dim.55), calls=%async_computation.1 | async-start | bytes 16384 | tf_op jit(solution)/shard_map/all_to_all | solution.py:17
  11.0 1.5 %reshape.922 = bf16[512,2,512]{2,1,0:T(2,128)(2,1)S(1)} reshape(bf16[1024,512]{1,0:T(8,128)(2,1)} %param.16) | data formatting | bytes 2097152 | tf_op jit(solution)/shard_map/reshape | solution.py:47
  12.5 1.5 %fusion.34 = (bf16[512,1,512]{2,1,0:T(2,128)(2,1)S(1)}, bf16[512,1,512]{2,1,0:T(2,128)(2,1)S(1)}) fusion(bf16[512,2,512]{2,1,0:T(2,128)(2,1)S(1)} %reshape.922), kind=kLoop, calls=%fused_computation.80 | loop fusion | bytes 2097152 | tf_op jit(solution)/shard_map/slice | solution.py:48
  14.0 1.5 %reshape.924 = bf16[512,2,512]{2,1,0:T(2,128)(2,1)S(1)} reshape(bf16[1024,512]{1,0:T(8,128)(2,1)} %param.18) | data formatting | bytes 2097152 | tf_op jit(solution)/shard_map/reshape | solution.py:47
  15.5 2.5 %fusion.35 = (bf16[512,1,512]{2,1,0:T(2,128)(2,1)}, bf16[512,1,512]{2,1,0:T(2,128)(2,1)}) fusion(bf16[512,2,512]{2,1,0:T(2,128)(2,1)S(1)} %reshape.924), kind=kLoop, calls=%fused_computation.81 | loop fusion | bytes 2097152 | tf_op jit(solution)/shard_map/slice | solution.py:48
  19.3 1.7 %reshape.926 = bf16[128,2,2048]{2,1,0:T(2,128)(2,1)S(1)} reshape(bf16[256,2048]{1,0:T(8,128)(2,1)} %param.20) | data formatting | bytes 2097152 | tf_op jit(solution)/shard_map/reshape | solution.py:47
  21.1 2.5 %fusion.36 = (bf16[128,1,2048]{2,1,0:T(2,128)(2,1)}, bf16[128,1,2048]{2,1,0:T(2,128)(2,1)}) fusion(bf16[128,2,2048]{2,1,0:T(2,128)(2,1)S(1)} %reshape.926), kind=kLoop, calls=%fused_computation.82 | loop fusion | bytes 2097152 | tf_op jit(solution)/shard_map/slice | solution.py:48
  23.8 14.3 %compare_select_fusion.1 = (bf16[128,1,2048]{2,0,1:T(8,128)(2,1)}, bf16[128,1,2048]{2,0,1:T(8,128)(2,1)}, bf16[128,1,2048]{2,0,1:T(8,128)(2,1)}, bf16[128,1,2048]{2,0,1:T(8,128)(2,1)}) fusion(s32[128]{0:T(128)S(1)} %rem.123, s32[16,2048]{1,0:T(8,128)S(1)} %copy-done.6, pred[16,2048]{1,0:T(8,128)(4,1)S(1)} %sign_compare_fusion, ...), kind=kLoop, calls=%fused_computation.40 | loop fusion | flops 7602176 | bytes 3310080 | tf_op jit(solution)/shard_map/jit(_where)/select_n | solution.py:52
  38.1 23.9 %bitcast_select_fusion.4 = (bf16[512,1,512]{2,0,1:T(8,128)(2,1)S(1)}, bf16[512,1,512]{2,0,1:T(8,128)(2,1)S(1)}, bf16[512,1,512]{2,0,1:T(8,128)(2,1)S(1)}, bf16[5...) fusion(s32[8]{0:T(128)S(1)} %copy-done.11, ...), kind=kLoop, calls=%fused_computation.28 | loop fusion | flops 15204352 | bytes 6619168 | tf_op jit(solution)/shard_map/jit(_where)/select_n | solution.py:52
  62.0 1.6 %pad_maximum_fusion = (bf16[512,4,512]{2,0,1:T(8,128)(2,1)S(1)}, bf16[512,4,512]{2,0,1:T(8,128)(2,1)}) fusion(bf16[512,1,512]{2,0,1:T(8,128)(2,1)S(1)} %get-tuple-element.23, bf16[512,1,512]{2,0,1:T(8,128)(2,1)S(1)} %get-tuple-element.25, bf16[512,1,512]{2,0,1:T(8,128)(2,1)S(1)} %get-tuple-element.26, bf16[512,1,512]{2,0,1:T(8,128)(2,1)S(1)} %get-tuple-element.24, ...), kind=kLoop, calls=%fused_computation.1 | loop fusion | flops 6291456 | bytes 8388608 | tf_op jit(solution)/shard_map/stack | solution.py:59
  63.6 1.6 %copy.48 = bf16[512,4,512]{2,1,0:T(4,128)(2,1)S(1)} copy(bf16[512,4,512]{2,0,1:T(8,128)(2,1)S(1)} %get-tuple-element.27) | data formatting | bytes 4194304 | tf_op jit(solution)/shard_map/stack | solution.py:59
  65.3 2.1 %reshape.923 = bf16[2048,512]{1,0:T(8,128)(2,1)} reshape(bf16[512,4,512]{2,1,0:T(4,128)(2,1)S(1)} %copy.48) | data formatting | bytes 4194304 | tf_op jit(solution)/shard_map/reshape | solution.py:60
  67.3 4.6 %copy.51 = bf16[512,4,512]{2,1,0:T(4,128)(2,1)} copy(bf16[512,4,512]{2,0,1:T(8,128)(2,1)} %get-tuple-element.28) | data formatting | bytes 4194304 | tf_op jit(solution)/shard_map/stack | solution.py:59
  71.9 2.6 %reshape.925 = bf16[2048,512]{1,0:T(8,128)(2,1)S(1)} reshape(bf16[512,4,512]{2,1,0:T(4,128)(2,1)} %copy.51) | data formatting | bytes 4194304 | tf_op jit(solution)/shard_map/reshape | solution.py:60
  75.3 7.3 %all-to-all-start = ((bf16[16,64,128]{2,1,0:T(8,128)(2,1)}), bf16[16,64,128]{2,1,0:T(8,128)(2,1)S(1)}, u32[]{:S(2)}, u32[]{:S(2)}) async-start(bf16[16,64,128]{2,1,0:T(8,128)(2,1)} %broadcast_in_dim.54), calls=%async_computation | async-start | bytes 524288 | tf_op jit(solution)/shard_map/all_to_all | solution.py:17
  82.6 1.5 %pad_maximum_fusion.2 = bf16[128,4,2048]{2,0,1:T(8,128)(2,1)S(1)} fusion(bf16[128,1,2048]{2,0,1:T(8,128)(2,1)} %get-tuple-element.16, bf16[128,1,2048]{2,0,1:T(8,128)(2,1)S(1)} %copy-done.3, bf16[128,1,2048]{2,0,1:T(8,128)(2,1)S(1)} %copy-done.2, bf16[128,1,2048]{2,0,1:T(8,128)(2,1)} %get-tuple-element.15), kind=kLoop, calls=%fused_computation.3 | loop fusion | flops 3145728 | bytes 4194304 | tf_op jit(solution)/shard_map/stack | solution.py:59
  84.0 3.0 %copy.54 = bf16[128,4,2048]{2,1,0:T(4,128)(2,1)} copy(bf16[128,4,2048]{2,0,1:T(8,128)(2,1)S(1)} %pad_maximum_fusion.2) | data formatting | bytes 4194304 | tf_op jit(solution)/shard_map/stack | solution.py:59
  87.0 3.9 %reshape.927 = bf16[512,2048]{1,0:T(8,128)(2,1)} reshape(bf16[128,4,2048]{2,1,0:T(4,128)(2,1)} %copy.54) | data formatting | bytes 4194304 | tf_op jit(solution)/shard_map/reshape | solution.py:60
  91.2 2.1 %fusion.15 = f32[64,512]{1,0:T(8,128)S(1)} fusion(bf16[2048,512]{1,0:T(8,128)(2,1)} %reshape.923, bf16[16,64,128]{2,1,0:T(8,128)(2,1)S(1)} %all-to-all-done, f32[16,128]{1,0:T(8,128)S(1)} %bitcast.111, f32[64]{0:T(128)S(1)} %add_rsqrt_fusion.1), kind=kOutput, calls=%fused_computation.53 | convolution fusion | flops 134742016 | bytes 2498816 | tf_op jit(solution)/shard_map/dot_general | solution.py:77
  93.3 2.6 %fusion = bf16[8,16,8,128]{3,2,1,0:T(8,128)(2,1)S(1)} fusion(bf16[512,2048]{1,0:T(8,128)(2,1)} %reshape.927, bf16[2048,512]{1,0:T(8,128)(2,1)S(1)} %reshape.925, f32[64,512]{1,0:T(8,128)S(1)} %fusion.15, bf16[16,64,128]{2,1,0:T(8,128)(2,1)S(1)} %all-to-all-done, f32[16,128]{1,0:T(8,128)S(1)} %bitcast.112, f32[64]{0:T(128)S(1)} %add_rsqrt_fusion.1), kind=kOutput, calls=%fused_computation.12 | convolution fusion | flops 269287424 | bytes 4858112 | tf_op jit(solution)/shard_map/dot_general | solution.py:81
  95.9 13.8 %all_to_all.22 = bf16[16,64,128]{2,1,0:T(8,128)(2,1)S(1)} all-to-all(bf16[16,64,128]{2,1,0:T(8,128)(2,1)S(1)} %bitcast.110), channel_id=1, replica_groups=mesh['dp'=32,'mp'=16] {'mp'}, dimensions={0} | all-to-all | bytes 524288 | tf_op jit(solution)/shard_map/all_to_all | solution.py:34
  110.5 5.3 %all-to-all-start.3 = ((f32[16,1,64]{2,1,0:T(1,128)}), f32[16,1,64]{2,1,0:T(1,128)S(1)}, u32[]{:S(2)}, u32[]{:S(2)}) async-start(f32[16,1,64]{2,1,0:T(1,128)} %broadcast_in_dim.62), calls=%async_computation.3 | async-start | bytes 16384 | tf_op jit(solution)/shard_map/all_to_all | solution.py:17
  115.9 6.1 %all-to-all-done.3 = f32[16,1,64]{2,1,0:T(1,128)S(1)} async-done(((f32[16,1,64]{2,1,0:T(1,128)}), f32[16,1,64]{2,1,0:T(1,128)S(1)}, u32[]{:S(2)}, u32[]{:S(2)}) %all-to-all-start.3) | async-done | bytes 4128 | tf_op jit(solution)/shard_map/all_to_all | solution.py:17
  (45 shorter events, 4.0 us)
Async XLA Ops:
  1.9 72.6 %all-to-all-start.1 = ((bf16[16,1,128]{2,1,0:T(2,128)(2,1)}), bf16[16,1,128]{2,1,0:T(2,128)(2,1)S(1)}, u32[]{:S(2)}, u32[]{:S(2)}) async-start(bf16[16,1,128]{2,1,0:T(2,128)(2,1)} %broadcast_in_dim.55), calls=%async_computation.1 | async-start | bytes 16384 | tf_op jit(solution)/shard_map/all_to_all | solution.py:17
  15.5 2.5 %copy-start.5 = (s32[64,512]{1,0:T(8,128)S(1)}, s32[64,512]{1,0:T(8,128)}, u32[]{:S(2)}) copy-start(s32[64,512]{1,0:T(8,128)} %param.17) | copy-start | bytes 393220
  15.5 3.2 %copy-start.4 = (s32[64,512]{1,0:T(8,128)S(1)}, s32[64,512]{1,0:T(8,128)}, u32[]{:S(2)}) copy-start(s32[64,512]{1,0:T(8,128)} %param.19) | copy-start | bytes 393220
  21.1 2.5 %copy-start.6 = (s32[16,2048]{1,0:T(8,128)S(1)}, s32[16,2048]{1,0:T(8,128)}, u32[]{:S(2)}) copy-start(s32[16,2048]{1,0:T(8,128)} %param.21) | copy-start | bytes 393220
  21.1 2.6 %copy-start.11 = (s32[8]{0:T(128)S(1)}, s32[8]{0:T(128)}, u32[]{:S(2)}) copy-start(s32[8]{0:T(128)} %constant.66.clone) | copy-start | bytes 100
  23.8 14.3 %copy-start = (bf16[512,1,512]{2,1,0:T(2,128)(2,1)S(1)}, bf16[512,1,512]{2,1,0:T(2,128)(2,1)}, u32[]{:S(2)}) copy-start(bf16[512,1,512]{2,1,0:T(2,128)(2,1)} %get-tuple-element.19) | copy-start | bytes 1572868
  23.8 14.3 %copy-start.1 = (bf16[512,1,512]{2,1,0:T(2,128)(2,1)S(1)}, bf16[512,1,512]{2,1,0:T(2,128)(2,1)}, u32[]{:S(2)}) copy-start(bf16[512,1,512]{2,1,0:T(2,128)(2,1)} %get-tuple-element.20) | copy-start | bytes 1572868
  23.8 14.3 %copy-start.7 = (pred[64,512]{1,0:T(8,128)(4,1)S(1)}, pred[64,512]{1,0:T(8,128)(4,1)}, u32[]{:S(2)}) copy-start(pred[64,512]{1,0:T(8,128)(4,1)} %fusion.27) | copy-start | bytes 98308
  23.8 14.3 %copy-start.8 = (pred[64,512]{1,0:T(8,128)(4,1)S(1)}, pred[64,512]{1,0:T(8,128)(4,1)}, u32[]{:S(2)}) copy-start(pred[64,512]{1,0:T(8,128)(4,1)} %fusion.28) | copy-start | bytes 98308
  71.9 2.7 %copy-start.9 = (bf16[64,128]{1,0:T(8,128)(2,1)S(1)}, bf16[64,128]{1,0:T(8,128)(2,1)}, u32[]{:S(2)}) copy-start(bf16[64,128]{1,0:T(8,128)(2,1)} %param.14) | copy-start | bytes 49156
  71.9 10.7 %copy-start.2 = (bf16[128,1,2048]{2,0,1:T(8,128)(2,1)S(1)}, bf16[128,1,2048]{2,0,1:T(8,128)(2,1)}, u32[]{:S(2)}) copy-start(bf16[128,1,2048]{2,0,1:T(8,128)(2,1)} %get-tuple-element.9) | copy-start | bytes 1572868
  71.9 10.7 %copy-start.3 = (bf16[128,1,2048]{2,0,1:T(8,128)(2,1)S(1)}, bf16[128,1,2048]{2,0,1:T(8,128)(2,1)}, u32[]{:S(2)}) copy-start(bf16[128,1,2048]{2,0,1:T(8,128)(2,1)} %get-tuple-element.10) | copy-start | bytes 1572868
  75.3 15.7 %all-to-all-start = ((bf16[16,64,128]{2,1,0:T(8,128)(2,1)}), bf16[16,64,128]{2,1,0:T(8,128)(2,1)S(1)}, u32[]{:S(2)}, u32[]{:S(2)}) async-start(bf16[16,64,128]{2,1,0:T(8,128)(2,1)} %broadcast_in_dim.54), calls=%async_computation | async-start | bytes 524288 | tf_op jit(solution)/shard_map/all_to_all | solution.py:17
  93.3 22.6 %copy-start.12 = (bf16[128]{0:T(256)(128)(2,1)S(1)}, bf16[128]{0:T(256)(128)(2,1)}, u32[]{:S(2)}) copy-start(bf16[128]{0:T(256)(128)(2,1)} %param.22) | copy-start | bytes 772
  109.9 12.8 %copy-start.10 = (bf16[64,128]{1,0:T(8,128)(2,1)}, bf16[64,128]{1,0:T(8,128)(2,1)S(1)}, u32[]{:S(2)}) copy-start(bf16[64,128]{1,0:T(8,128)(2,1)S(1)} %get-tuple-element.4) | copy-start | bytes 49156
  110.5 11.5 %all-to-all-start.3 = ((f32[16,1,64]{2,1,0:T(1,128)}), f32[16,1,64]{2,1,0:T(1,128)S(1)}, u32[]{:S(2)}, u32[]{:S(2)}) async-start(f32[16,1,64]{2,1,0:T(1,128)} %broadcast_in_dim.62), calls=%async_computation.3 | async-start | bytes 16384 | tf_op jit(solution)/shard_map/all_to_all | solution.py:17
where the time goes:
time: 123 us
  other arithmetic  43.6 us (35%)
  local copies, waits for them, and re-layouts  31.8 us (26%)
  starting transfers between devices  21.8 us (18%)
  blocking collectives  13.8 us (11%)
  waiting for transfers between devices  6.14 us (5%)
  matrix products  4.67 us (4%)
    select_n x2, other arithmetic, expand(): jnp.where(digits == 0, second_val, jnp.where((digits == 3) | (digits == 4...  38.2 us
    all_to_all x3, starting transfers between devices, from_everyone(): lax.all_to_all(jnp.broadcast_to(array[None], (size, *array.shape)), axis,...  21.8 us
    all_to_all x1, blocking collectives, sum_at_owner(): parts = lax.all_to_all(cut_along(array, dim, size), axis, 0, 0, tiled=True)  13.8 us
    another operation x3, local copies, waits for them, and re-layouts, expand(): dense = jnp.stack([row_zero, row_one, row_two, row_three], axis=1)  9.15 us
    reshape x3, local copies, waits for them, and re-layouts, expand(): return dense.reshape(digits.shape[0] * 4, values.shape[1])  8.63 us
    slice x3, local copies, waits for them, and re-layouts, expand(): first_val = paired[:, 0, :]  6.51 us
    all_to_all x3, waiting for transfers between devices, from_everyone(): lax.all_to_all(jnp.broadcast_to(array[None], (size, *array.shape)), axis,...  6.14 us
    reshape x3, local copies, waits for them, and re-layouts, expand(): paired = values.reshape(digits.shape[0], 2, values.shape[1])  4.68 us
  transfers between devices with their start and end apart: 3, of which 1 were waited for; matrix products, arithmetic and copies ran while one was open for 58% of the time, Pallas kernels for 0%

commit v1 on v0

v1 whole, which is shorter than its diff:
```python
import functools

import jax
import jax.numpy as jnp
from jax import lax
from jax.experimental import pallas as pl
from jax.experimental.pallas import tpu as pltpu
from jax.sharding import PartitionSpec as P

MESH = pl.DeviceIdType.MESH
F32 = jnp.float32
BF16 = jnp.bfloat16
epsilon = 1e-05


def iota(shape, dim):
    return lax.broadcasted_iota(jnp.int32, shape, dim)


def decode_rows(vals, mask, width):
    row = iota((16, 1), 0)
    digit = row // 2
    odd = row % 2 == 1
    scale = jnp.zeros((16, 1), F32)
    for k in range(8):
        scale = jnp.where(digit == k, F32(1.0 / 6 ** (k + 1)), scale)
    scale = jnp.broadcast_to(scale, (16, 128))
    odd = jnp.broadcast_to(odd, (16, 128))
    first_top = jnp.where(odd, F32(1), F32(3))
    second_low = jnp.where(odd, F32(4), F32(5))
    middle = jnp.where(odd, F32(2.5), F32(100))
    zero = jnp.zeros((16, 128), F32)
    uppers, lowers = [], []
    for c in range(width // 128):
        lanes = slice(c * 128, c * 128 + 128)
        packed = jnp.broadcast_to(mask[:, lanes], (16, 128))
        turn = packed * scale
        place = (turn - jnp.floor(turn)) * F32(6)
        kept = vals[:, lanes].astype(F32)
        in_upper = place < first_top
        in_lower = (place > second_low) | (jnp.abs(place - middle) < F32(0.5))
        upper = jnp.where(in_upper, kept, zero)
        lower = jnp.where(in_lower, kept, zero)
        crossing = jnp.where(in_upper | in_lower, zero, kept)
        down = jnp.concatenate(
            [pltpu.roll(crossing[:8], 1, 0), pltpu.roll(crossing[8:], 1, 0)], axis=0
        )
        up = jnp.concatenate(
            [pltpu.roll(crossing[:8], 7, 0), pltpu.roll(crossing[8:], 7, 0)], axis=0
        )
        upper = jnp.where(odd, upper + down, upper)
        lower = jnp.where(odd, lower, lower + up)
        uppers.append(upper.astype(BF16))
        lowers.append(lower.astype(BF16))
    return jnp.concatenate(uppers, axis=1), jnp.concatenate(lowers, axis=1)


def permutation():
    source, target = iota((128, 128), 0), iota((128, 128), 1)
    q = target % 32
    order = target // 32 * 32 + (q % 16) // 2 * 4 + q % 2 + q // 16 * 2
    return jnp.where(source == order, F32(1), F32(0)).astype(BF16)


def row_sums_tile(values, eye):
    sums = jnp.sum(values, axis=1, keepdims=True)
    spread = jnp.where(eye, sums, F32(0))
    tile = spread[0:8]
    for v in range(1, 8):
        tile = tile + spread[8 * v : 8 * v + 8]
    return tile


def row_column(tile, eye):
    spread = jnp.where(eye, jnp.concatenate([tile] * 8, axis=0), F32(0))
    return jnp.sum(spread, axis=1, keepdims=True)


def kernel(
    n,
    ny,
    x_ref,
    ngain_ref,
    fgain_ref,
    gv_hbm,
    gm_hbm,
    uv_hbm,
    um_hbm,
    dv_hbm,
    dm_hbm,
    so_ref,
    fn_ref,
    gv,
    uv,
    dv,
    gm,
    um,
    dm,
    wgu,
    wd,
    acc,
    xbuf,
    part,
    rbuf,
    sbuf,
    load_sem,
    xs_sem,
    xr_sem,
    ps_sem,
    pr_sem,
    ss_sem,
    sr_sem,
):
    me = lax.axis_index("mp")
    nx = n // ny
    mx, my = me // ny, me % ny
    barrier = pltpu.get_barrier_semaphore()
    for step in range(1, n):
        peer = lax.rem(me + step, n)
        pl.semaphore_signal(barrier, inc=1, device_id={"mp": peer}, device_id_type=MESH)
    loads = [
        pltpu.make_async_copy(src, dst, load_sem.at[i])
        for i, (src, dst) in enumerate(
            [(gm_hbm, gm), (gv_hbm, gv), (um_hbm, um), (uv_hbm, uv), (dm_hbm, dm), (dv_hbm, dv)]
        )
    ]
    for load in loads:
        load.start()

    eye = iota((64, 128), 0) == iota((64, 128), 1)
    perm = permutation()
    x = x_ref[...].astype(F32)
    gained = (x * ngain_ref[...].astype(F32)).astype(BF16)
    gained = jnp.dot(gained, perm, preferred_element_type=F32).astype(BF16)
    tile = row_sums_tile(x * x, eye)
    high = tile.astype(BF16)
    rest = (tile - high.astype(F32)).astype(BF16)
    xbuf[me, 0:64, :] = gained
    xbuf[me, 64:80, :] = jnp.concatenate([high, rest], axis=0)

    pairs = []
    for dx in [2, 1, 3, 0]:
        for dy in [1, 0]:
            pairs.append(lax.rem(mx + dx, nx) * 2 + lax.rem(my // 2 + dy, 2))
    peers = []
    for pair in pairs[:-1]:
        peers += [2 * pair, 2 * pair + 1]
    peers.append(me + 1 - 2 * lax.rem(me, 2))

    def copies(src, dst, send, recv):
        out = []
        for peer in peers:
            out.append(
                (
                    pltpu.make_async_remote_copy(
                        src_ref=src(peer),
                        dst_ref=dst.at[me],
                        send_sem=send.at[peer],
                        recv_sem=recv.at[me],
                        device_id={"mp": peer},
                        device_id_type=MESH,
                    )
                )
            )
        return out

    def arrival(peer, dst, send, recv):
        return pltpu.make_async_remote_copy(
            src_ref=dst.at[peer],
            dst_ref=dst.at[peer],
            send_sem=send.at[peer],
            recv_sem=recv.at[peer],
            device_id={"mp": peer},
            device_id_type=MESH,
        )

    pl.semaphore_wait(barrier, n - 1)
    x_sends = copies(lambda peer: xbuf.at[me], xbuf, xs_sem, xr_sem)
    for send in x_sends:
        send.start()

    def decode_gate_up(vals, mask, at):
        def body(i, carry):
            row = mask[pl.ds(i, 1), :].astype(F32) + F32(0.5)
            rows = vals[pl.ds(pl.multiple_of(i * 16, 16), 16), :]
            upper, lower = decode_rows(rows, row, 512)
            start = pl.multiple_of(i * 32, 32)
            wgu[pl.ds(start, 16), at : at + 512] = upper
            wgu[pl.ds(start + 16, 16), at : at + 512] = lower
            return carry

        lax.fori_loop(0, 64, body, 0)

    loads[0].wait()
    loads[1].wait()
    decode_gate_up(gv, gm, 0)
    loads[2].wait()
    loads[3].wait()
    decode_gate_up(uv, um, 512)
    loads[4].wait()
    loads[5].wait()

    def decode_down(i, carry):
        for c in range(4):
            lanes = slice(c * 512, c * 512 + 512)
            row = dm[pl.ds(i, 1), lanes].astype(F32) + F32(0.5)
            rows = dv[pl.ds(pl.multiple_of(i * 16, 16), 16), lanes]
            upper, lower = decode_rows(rows, row, 512)
            start = pl.multiple_of(i * 32, 32)
            wd[pl.ds(start, 16), lanes] = upper
            wd[pl.ds(start + 16, 16), lanes] = lower
        return carry

    lax.fori_loop(0, 16, decode_down, 0)

    total = None
    for index, pair in enumerate(pairs[::-1]):
        if index == 0:
            arrival(peers[-1], xbuf, xs_sem, xr_sem).wait_recv()
        else:
            arrival(2 * pair, xbuf, xs_sem, xr_sem).wait_recv()
            arrival(2 * pair + 1, xbuf, xs_sem, xr_sem).wait_recv()
        left, right = xbuf[2 * pair], xbuf[2 * pair + 1]
        block = jnp.concatenate([left[0:64], right[0:64]], axis=1)
        for side in (left, right):
            tile = side[64:72].astype(F32) + side[72:80].astype(F32)
            total = tile if total is None else total + tile
        depth = pl.ds(pl.multiple_of(pair * 256, 256), 256)
        for c in range(2):
            lanes = slice(c * 512, c * 512 + 512)
            product = jnp.dot(block, wgu[depth, lanes], preferred_element_type=F32)
            if index == 0:
                acc[:, lanes] = product
            else:
                acc[:, lanes] += product

    scale = lax.rsqrt(row_column(total, eye) / F32(n * 128) + F32(epsilon))
    gate = acc[:, 0:512] * scale
    up = acc[:, 512:1024] * scale
    hidden = (jax.nn.silu(gate) * up).astype(BF16)
    hidden = jnp.concatenate(
        [
            jnp.dot(hidden[:, c * 128 : c * 128 + 128], perm, preferred_element_type=F32)
            for c in range(4)
        ],
        axis=1,
    ).astype(BF16)

    p_sends = copies(lambda peer: part.at[peer], rbuf, ps_sem, pr_sem)
    for index, pair in enumerate(pairs):
        lanes = pl.ds(pl.multiple_of(pair * 256, 256), 256)
        product = jnp.dot(hidden, wd[:, lanes], preferred_element_type=F32).astype(BF16)
        part[2 * pair] = product[:, 0:128]
        part[2 * pair + 1] = product[:, 128:256]
        for send in p_sends[2 * index : 2 * index + 2]:
            send.start()

    summed = part[me].astype(F32)
    for peer in peers[::-1]:
        arrival(peer, rbuf, ps_sem, pr_sem).wait_recv()
        summed += rbuf[peer].astype(F32)
    out = (x_ref[...].astype(F32) + summed).astype(BF16)
    so_ref[...] = out
    out = out.astype(F32)
    sbuf[me] = row_sums_tile(out * out, eye)
    s_sends = copies(lambda peer: sbuf.at[me], sbuf, ss_sem, sr_sem)
    for send in s_sends:
        send.start()
    total = sbuf[me]
    for peer in peers[::-1]:
        arrival(peer, sbuf, ss_sem, sr_sem).wait_recv()
        total += sbuf[peer]
    scale = lax.rsqrt(row_column(total, eye) / F32(n * 128) + F32(epsilon))
    fn_ref[...] = (out * scale * fgain_ref[...].astype(F32)).astype(BF16)
    for send in x_sends + p_sends + s_sends:
        send.wait_send()


def solution(mesh):
    n = mesh.shape["mp"]
    vmem = pl.BlockSpec(memory_space=pltpu.VMEM)
    hbm = pl.BlockSpec(memory_space=pl.ANY)

    def step(stream, ngain, gv, gm, uv, um, dv, dm, fgain):
        block = jax.ShapeDtypeStruct(stream.shape, BF16)
        dma = pltpu.SemaphoreType.DMA
        return pl.pallas_call(
            functools.partial(kernel, n, 4),
            out_shape=(block, block),
            in_specs=[vmem] * 3 + [hbm] * 6,
            out_specs=(vmem, vmem),
            scratch_shapes=[
                pltpu.VMEM(gv.shape, BF16),
                pltpu.VMEM(uv.shape, BF16),
                pltpu.VMEM(dv.shape, BF16),
                pltpu.VMEM(gm.shape, jnp.int32),
                pltpu.VMEM(um.shape, jnp.int32),
                pltpu.VMEM(dm.shape, jnp.int32),
                pltpu.VMEM((2048, 1024), BF16),
                pltpu.VMEM((512, 2048), BF16),
                pltpu.VMEM((64, 1024), F32),
                pltpu.VMEM((n, 80, 128), BF16),
                pltpu.VMEM((n, 64, 128), BF16),
                pltpu.VMEM((n, 64, 128), BF16),
                pltpu.VMEM((n, 8, 128), F32),
                dma((6,)),
                dma((n,)),
                dma((n,)),
                dma((n,)),
                dma((n,)),
                dma((n,)),
                dma((n,)),
            ],
            compiler_params=pltpu.CompilerParams(collective_id=0, has_side_effects=True),
        )(stream, ngain.reshape(1, -1), fgain.reshape(1, -1), gv, gm, uv, um, dv, dm)

    cols = P(None, "mp")
    return jax.shard_map(
        step,
        mesh=mesh,
        in_specs=(
            P("dp", "mp"),
            P("mp"),
            cols,
            cols,
            cols,
            cols,
            P("mp", None),
            P("mp", None),
            P("mp"),
        ),
        out_specs=(P("dp", "mp"), P("dp", "mp")),
        check_vma=False,
    )
```

time: 123 us -> 30.4 us (0.25)
  other arithmetic: 43.6 us -> 0 us
  local copies, waits for them, and re-layouts: 31.8 us -> 1.94 us
  Pallas kernels: 0 us -> 27.6 us
  starting transfers between devices: 21.8 us -> 0 us
  blocking collectives: 13.8 us -> 0 us
  waiting for transfers between devices: 6.14 us -> 0 us
  matrix products: 4.67 us -> 0 us
    select_n x2 -> x0, other arithmetic: 38.2 us -> none  [expand(): jnp.where(digits == 0, second_val, jnp.where((digits == 3) | (digits == 4...]
    pallas_call x0 -> x1, Pallas kernels: none -> 27.6 us  [step(): pl.pallas_call(functools.partial(kernel, n, 4), out_shape=(block, block),...]
    all_to_all x3 -> x0, starting transfers between devices: 21.8 us -> none  [from_everyone(): lax.all_to_all(jnp.broadcast_to(array[None], (size, *array.shape)), axis,...]
    all_to_all x1 -> x0, blocking collectives: 13.8 us -> none  [sum_at_owner(): parts = lax.all_to_all(cut_along(array, dim, size), axis, 0, 0, tiled=True)]
    reshape x7 -> x0, local copies, waits for them, and re-layouts: 13.4 us -> none  [the longest x3 8.63 us: expand(): return dense.reshape(digits.shape[0] * 4, values.shape[1])]
    another operation x3 -> x0, local copies, waits for them, and re-layouts: 9.15 us -> none  [expand(): dense = jnp.stack([row_zero, row_one, row_two, row_three], axis=1)]
    slice x3 -> x0, local copies, waits for them, and re-layouts: 6.51 us -> none  [expand(): first_val = paired[:, 0, :]]
    all_to_all x3 -> x0, waiting for transfers between devices: 6.14 us -> none  [from_everyone(): lax.all_to_all(jnp.broadcast_to(array[None], (size, *array.shape)), axis,...]
  transfers between devices with their start and end apart: 3 -> 0, of which waited for: 1 -> 0; matrix products, arithmetic and copies ran while one was open for 58% -> 0% of each run, Pallas kernels for 0% -> 0%
where the time goes in v1:
time: 30.4 us; the launch traced here: 30.2 us
  Pallas kernels  27.6 us (91%)
  local copies, waits for them, and re-layouts  1.94 us (6%)
  between operations  0.65 us (2%)
    pallas_call x1, Pallas kernels, step(): pl.pallas_call(functools.partial(kernel, n, 4), out_shape=(block, block),...  27.6 us
    unnamed x4, local copies, waits for them, and re-layouts  1.94 us

profile of v1, /device:TPU:2, one launch (start us, length us, event | category | flops | bytes accessed | tf_op | source)
XLA Modules:
  0.0 30.2 jit_solution(14101797383458763729)
XLA Ops:
  0.6 27.6 %shard_map.104 = (bf16[64,128]{1,0:T(8,128)(2,1)}, bf16[64,128]{1,0:T(8,128)(2,1)}) custom-call(bf16[64,128]{1,0:T(8,128)(2,1)} %x_ref.1, bf16[1,128]{1,0:T(2,128)(2,1)} %bitcast.2, bf16[1,128]{1,0:T(2,128)(2,1)} %bitcast.3, bf16[1024,512]{1,0:T(8,128)(2,1)} %gv_hbm.1, s32[64,512]{1,0:T(8,128)} %gm_hbm.1, bf16[1024,512]{1,0:T(8,128)(2,1)} %uv_hbm.1, ...), custom_call_target="tpu_custom_call" | custom-call | tf_op jit(solution)/shard_map/pallas_call | solution.py:287
  28.3 0.0 copy-start
  28.3 1.3 %copy.13 = bf16[64,128]{1,0:T(8,128)(2,1)} copy(bf16[64,128]{1,0:T(8,128)(2,1)} %get-tuple-element.4) | data formatting | bytes 32768
  29.6 0.0 copy-done
  29.6 0.6 %copy.14 = bf16[64,128]{1,0:T(8,128)(2,1)} copy(bf16[64,128]{1,0:T(8,128)(2,1)S(1)} %copy-done) | data formatting | bytes 32768
Async XLA Ops:
  28.3 1.3 %copy-start = (bf16[64,128]{1,0:T(8,128)(2,1)S(1)}, bf16[64,128]{1,0:T(8,128)(2,1)}, u32[]{:S(2)}) copy-start(bf16[64,128]{1,0:T(8,128)(2,1)} %get-tuple-element.5) | copy-start | bytes 49156

commit v2 on v1

--- a/solution.py
+++ b/solution.py
@@ -62,26 +62,22 @@
     return jnp.where(source == order, F32(1), F32(0)).astype(BF16)
 
 
-def row_sums_tile(values, eye):
+def row_sums(values, eye):
     sums = jnp.sum(values, axis=1, keepdims=True)
-    spread = jnp.where(eye, sums, F32(0))
-    tile = spread[0:8]
-    for v in range(1, 8):
-        tile = tile + spread[8 * v : 8 * v + 8]
-    return tile
-
-
-def row_column(tile, eye):
-    spread = jnp.where(eye, jnp.concatenate([tile] * 8, axis=0), F32(0))
-    return jnp.sum(spread, axis=1, keepdims=True)
+    return jnp.sum(jnp.where(eye, sums, F32(0)), axis=0, keepdims=True)
+
+
+def row_column(rows, eye):
+    total = jnp.sum(rows[:, 0, :], axis=0, keepdims=True)
+    return jnp.sum(jnp.where(eye, total, F32(0)), axis=1, keepdims=True)
 
 
 def kernel(
     n,
     ny,
-    x_ref,
-    ngain_ref,
-    fgain_ref,
+    x_hbm,
+    ngain_hbm,
+    fgain_hbm,
     gv_hbm,
     gm_hbm,
     uv_hbm,
@@ -90,6 +86,9 @@
     dm_hbm,
     so_ref,
     fn_ref,
+    x_ref,
+    ngain_ref,
+    fgain_ref,
     gv,
     uv,
     dv,
@@ -100,12 +99,15 @@
     wd,
     acc,
     xbuf,
+    qbuf,
     part,
     rbuf,
     sbuf,
     load_sem,
     xs_sem,
     xr_sem,
+    qs_sem,
+    qr_sem,
     ps_sem,
     pr_sem,
     ss_sem,
@@ -121,7 +123,16 @@
     loads = [
         pltpu.make_async_copy(src, dst, load_sem.at[i])
         for i, (src, dst) in enumerate(
-            [(gm_hbm, gm), (gv_hbm, gv), (um_hbm, um), (uv_hbm, uv), (dm_hbm, dm), (dv_hbm, dv)]
+            [
+                (x_hbm, x_ref),
+                (ngain_hbm, ngain_ref),
+                (fgain_hbm, fgain_ref),
+                (gm_hbm, gm), (gv_hbm, gv),
+                (um_hbm, um),
+                (uv_hbm, uv),
+                (dm_hbm, dm),
+                (dv_hbm, dv),
+            ]
         )
     ]
     for load in loads:
@@ -129,14 +140,12 @@
 
     eye = iota((64, 128), 0) == iota((64, 128), 1)
     perm = permutation()
+    for load in loads[:3]:
+        load.wait()
     x = x_ref[...].astype(F32)
     gained = (x * ngain_ref[...].astype(F32)).astype(BF16)
-    gained = jnp.dot(gained, perm, preferred_element_type=F32).astype(BF16)
-    tile = row_sums_tile(x * x, eye)
-    high = tile.astype(BF16)
-    rest = (tile - high.astype(F32)).astype(BF16)
-    xbuf[me, 0:64, :] = gained
-    xbuf[me, 64:80, :] = jnp.concatenate([high, rest], axis=0)
+    xbuf[me] = jnp.dot(gained, perm, preferred_element_type=F32).astype(BF16)
+    qbuf[me] = row_sums(x * x, eye)
 
     pairs = []
     for dx in [2, 1, 3, 0]:
@@ -176,7 +185,8 @@
 
     pl.semaphore_wait(barrier, n - 1)
     x_sends = copies(lambda peer: xbuf.at[me], xbuf, xs_sem, xr_sem)
-    for send in x_sends:
+    q_sends = copies(lambda peer: qbuf.at[me], qbuf, qs_sem, qr_sem)
+    for send in x_sends + q_sends:
         send.start()
 
     def decode_gate_up(vals, mask, at):
@@ -191,14 +201,14 @@
 
         lax.fori_loop(0, 64, body, 0)
 
-    loads[0].wait()
-    loads[1].wait()
+    loads[3].wait()
+    loads[4].wait()
     decode_gate_up(gv, gm, 0)
-    loads[2].wait()
-    loads[3].wait()
+    loads[5].wait()
+    loads[6].wait()
     decode_gate_up(uv, um, 512)
-    loads[4].wait()
-    loads[5].wait()
+    loads[7].wait()
+    loads[8].wait()
 
     def decode_down(i, carry):
         for c in range(4):
@@ -213,18 +223,13 @@
 
     lax.fori_loop(0, 16, decode_down, 0)
 
-    total = None
     for index, pair in enumerate(pairs[::-1]):
         if index == 0:
             arrival(peers[-1], xbuf, xs_sem, xr_sem).wait_recv()
         else:
             arrival(2 * pair, xbuf, xs_sem, xr_sem).wait_recv()
             arrival(2 * pair + 1, xbuf, xs_sem, xr_sem).wait_recv()
-        left, right = xbuf[2 * pair], xbuf[2 * pair + 1]
-        block = jnp.concatenate([left[0:64], right[0:64]], axis=1)
-        for side in (left, right):
-            tile = side[64:72].astype(F32) + side[72:80].astype(F32)
-            total = tile if total is None else total + tile
+        block = jnp.concatenate([xbuf[2 * pair], xbuf[2 * pair + 1]], axis=1)
         depth = pl.ds(pl.multiple_of(pair * 256, 256), 256)
         for c in range(2):
             lanes = slice(c * 512, c * 512 + 512)
@@ -234,7 +239,9 @@
             else:
                 acc[:, lanes] += product
 
-    scale = lax.rsqrt(row_column(total, eye) / F32(n * 128) + F32(epsilon))
+    for peer in peers[::-1]:
+        arrival(peer, qbuf, qs_sem, qr_sem).wait_recv()
+    scale = lax.rsqrt(row_column(qbuf[...], eye) / F32(n * 128) + F32(epsilon))
     gate = acc[:, 0:512] * scale
     up = acc[:, 512:1024] * scale
     hidden = (jax.nn.silu(gate) * up).astype(BF16)
@@ -260,19 +267,17 @@
         arrival(peer, rbuf, ps_sem, pr_sem).wait_recv()
         summed += rbuf[peer].astype(F32)
     out = (x_ref[...].astype(F32) + summed).astype(BF16)
+    out = out.astype(F32)
     so_ref[...] = out
-    out = out.astype(F32)
-    sbuf[me] = row_sums_tile(out * out, eye)
+    sbuf[me] = row_sums(out * out, eye)
     s_sends = copies(lambda peer: sbuf.at[me], sbuf, ss_sem, sr_sem)
     for send in s_sends:
         send.start()
-    total = sbuf[me]
     for peer in peers[::-1]:
         arrival(peer, sbuf, ss_sem, sr_sem).wait_recv()
-        total += sbuf[peer]
-    scale = lax.rsqrt(row_column(total, eye) / F32(n * 128) + F32(epsilon))
-    fn_ref[...] = (out * scale * fgain_ref[...].astype(F32)).astype(BF16)
-    for send in x_sends + p_sends + s_sends:
+    scale = lax.rsqrt(row_column(sbuf[...], eye) / F32(n * 128) + F32(epsilon))
+    fn_ref[...] = scale * fgain_ref[...].astype(F32)
+    for send in x_sends + q_sends + p_sends + s_sends:
         send.wait_send()
 
 
@@ -282,14 +287,17 @@
     hbm = pl.BlockSpec(memory_space=pl.ANY)
 
     def step(stream, ngain, gv, gm, uv, um, dv, dm, fgain):
-        block = jax.ShapeDtypeStruct(stream.shape, BF16)
+        block = pltpu.VMEM(stream.shape, F32)
         dma = pltpu.SemaphoreType.DMA
-        return pl.pallas_call(
+        out, factor = pl.pallas_call(
             functools.partial(kernel, n, 4),
             out_shape=(block, block),
-            in_specs=[vmem] * 3 + [hbm] * 6,
+            in_specs=[hbm] * 9,
             out_specs=(vmem, vmem),
             scratch_shapes=[
+                pltpu.VMEM(stream.shape, BF16),
+                pltpu.VMEM((1, 128), BF16),
+                pltpu.VMEM((1, 128), BF16),
                 pltpu.VMEM(gv.shape, BF16),
                 pltpu.VMEM(uv.shape, BF16),
                 pltpu.VMEM(dv.shape, BF16),
@@ -299,11 +307,14 @@
                 pltpu.VMEM((2048, 1024), BF16),
                 pltpu.VMEM((512, 2048), BF16),
                 pltpu.VMEM((64, 1024), F32),
-                pltpu.VMEM((n, 80, 128), BF16),
+                pltpu.VMEM((n, 64, 128), BF16),
+                pltpu.VMEM((n, 1, 128), F32),
                 pltpu.VMEM((n, 64, 128), BF16),
                 pltpu.VMEM((n, 64, 128), BF16),
-                pltpu.VMEM((n, 8, 128), F32),
-                dma((6,)),
+                pltpu.VMEM((n, 1, 128), F32),
+                dma((9,)),
+                dma((n,)),
+                dma((n,)),
                 dma((n,)),
                 dma((n,)),
                 dma((n,)),
@@ -313,6 +324,7 @@
             ],
             compiler_params=pltpu.CompilerParams(collective_id=0, has_side_effects=True),
         )(stream, ngain.reshape(1, -1), fgain.reshape(1, -1), gv, gm, uv, um, dv, dm)
+        return out.astype(BF16), (out * factor).astype(BF16)
 
     cols = P(None, "mp")
     return jax.shard_map(

time: 30.4 us -> 28.1 us (0.924)
  local copies, waits for them, and re-layouts: 1.94 us -> 0 us
  Pallas kernels: 27.6 us -> 26.6 us
  other arithmetic: 0 us -> 0.62 us
    unnamed x4 -> x0, local copies, waits for them, and re-layouts: 1.94 us -> none
    pallas_call x1, Pallas kernels: 27.6 us -> 26.6 us  [step(): pl.pallas_call(functools.partial(kernel, n, 4), out_shape=(block, block),...]
    convert_element_type x0 -> x1, other arithmetic: none -> 0.62 us  [step(): return (out.astype(BF16), (out * factor).astype(BF16))]
where the time goes in v2:
time: 28.1 us; the launch traced here: 27.9 us
  Pallas kernels  26.6 us (95%)
  between operations  0.64 us (2%)
  other arithmetic  0.62 us (2%)
    pallas_call x1, Pallas kernels, step(): pl.pallas_call(functools.partial(kernel, n, 4), out_shape=(block, block),...  26.6 us
    convert_element_type x1, other arithmetic, step(): return (out.astype(BF16), (out * factor).astype(BF16))  0.62 us

profile of v2, /device:TPU:2, one launch (start us, length us, event | category | flops | bytes accessed | tf_op | source)
XLA Modules:
  0.0 27.9 jit_solution(3565020577025240600)
XLA Ops:
  0.6 26.6 %shard_map.104 = (f32[64,128]{1,0:T(8,128)S(1)}, f32[64,128]{1,0:T(8,128)S(1)}) custom-call(bf16[64,128]{1,0:T(8,128)(2,1)} %x_hbm.1, bf16[1,128]{1,0:T(2,128)(2,1)} %bitcast.2, bf16[1,128]{1,0:T(2,128)(2,1)} %bitcast.3, bf16[1024,512]{1,0:T(8,128)(2,1)} %gv_hbm.1, s32[64,512]{1,0:T(8,128)} %gm_hbm.1, bf16[1024,512]{1,0:T(8,128)(2,1)} %uv_hbm.1, ...), custom_call_target="tpu_custom_call" | custom-call | tf_op jit(solution)/shard_map/pallas_call | solution.py:292
  27.3 0.6 %multiply_convert_fusion = (bf16[64,128]{1,0:T(8,128)(2,1)}, bf16[64,128]{1,0:T(8,128)(2,1)}) fusion(f32[64,128]{1,0:T(8,128)S(1)} %get-tuple-element.4, f32[64,128]{1,0:T(8,128)S(1)} %get-tuple-element.5), kind=kLoop, calls=%fused_computation | loop fusion | flops 24576 | bytes 98304 | tf_op jit(solution)/shard_map/convert_element_type | solution.py:327

commit v3 on v2

v3 whole, which is shorter than its diff:
```python
import functools

import jax
import jax.numpy as jnp
from jax import lax
from jax.experimental import pallas as pl
from jax.experimental.pallas import tpu as pltpu
from jax.sharding import PartitionSpec as P

MESH = pl.DeviceIdType.MESH
F32 = jnp.float32
BF16 = jnp.bfloat16
epsilon = 1e-05


def iota(shape, dim):
    return lax.broadcasted_iota(jnp.int32, shape, dim)


def sublanes(array, index):
    return jnp.take_along_axis(array, index, axis=0, mode="promise_in_bounds")


def decode_rows(vals, mask, width):
    group = iota((8, 128), 0)
    scale = jnp.zeros((8, 128), F32)
    for k in range(8):
        scale = jnp.where(group == k, F32(1.0 / 6 ** (k + 1)), scale)
    row = iota((16, 128), 0)
    odd = (row - row // 2 * 2).astype(F32).astype(BF16)
    second = odd > BF16(0.5)
    upper_top = BF16(3) - BF16(2) * odd
    lower_low = BF16(4.5) - odd
    lower_also = BF16(9) - BF16(7) * odd
    zero = jnp.zeros((16, 128), BF16)
    other = group + 1 - 2 * (group - group // 2 * 2)
    uppers, lowers = [], []
    for c in range(width // 128):
        lanes = slice(c * 128, c * 128 + 128)
        turn = jnp.broadcast_to(mask[:, lanes], (8, 128)) * scale
        digit = jnp.floor((turn - jnp.floor(turn)) * F32(6))
        digit = jnp.concatenate(
            [sublanes(digit, group // 2), sublanes(digit, group // 2 + 4)], axis=0
        ).astype(BF16)
        kept = vals[:, lanes]
        in_upper = digit < upper_top
        in_lower = (digit > lower_low) | (digit == lower_also)
        crossing = jnp.where(in_upper | in_lower, zero, kept).astype(F32)
        crossed = jnp.concatenate(
            [sublanes(crossing[:8], other), sublanes(crossing[8:], other)], axis=0
        ).astype(BF16)
        uppers.append(jnp.where(in_upper, kept, jnp.where(second, crossed, zero)))
        lowers.append(jnp.where(in_lower, kept, jnp.where(second, zero, crossed)))
    return jnp.concatenate(uppers, axis=1), jnp.concatenate(lowers, axis=1)


def column_order(shape):
    target = iota(shape, 1)
    q = target % 32
    return target // 32 * 32 + (q % 16) // 2 * 4 + q % 2 + q // 16 * 2


def row_sums(values, eye):
    sums = jnp.sum(values, axis=1, keepdims=True)
    return jnp.sum(jnp.where(eye, sums, F32(0)), axis=0, keepdims=True)


def row_column(row, eye):
    return jnp.sum(jnp.where(eye, row, F32(0)), axis=1, keepdims=True)


def kernel(
    n,
    ny,
    x_hbm,
    ngain_hbm,
    fgain_hbm,
    gv_hbm,
    gm_hbm,
    uv_hbm,
    um_hbm,
    dv_hbm,
    dm_hbm,
    so_ref,
    fn_ref,
    x_ref,
    ngain_ref,
    fgain_ref,
    gv,
    uv,
    dv,
    gm,
    um,
    dm,
    wgu,
    wd,
    acc,
    xbuf,
    part,
    rbuf,
    sbuf,
    load_sem,
    xs_sem,
    xr_sem,
    ps_sem,
    pr_sem,
    ss_sem,
    sr_sem,
):
    me = lax.axis_index("mp")
    nx = n // ny
    mx, my = me // ny, me % ny
    loads = [
        pltpu.make_async_copy(src, dst, load_sem.at[i])
        for i, src, dst in [
            (0, x_hbm, x_ref),
            (0, ngain_hbm, ngain_ref),
            (1, gm_hbm, gm),
            (1, gv_hbm, gv),
            (1, um_hbm, um),
            (1, uv_hbm, uv),
            (2, dm_hbm, dm),
            (2, dv_hbm, dv),
            (2, fgain_hbm, fgain_ref),
        ]
    ]
    for load in loads[:2]:
        load.start()
    barrier = pltpu.get_barrier_semaphore()
    peers = [
        lax.rem(mx + dx, nx) * ny + lax.rem(my + dy, ny)
        for dx, dy in [
            (2, 2), (2, 1), (1, 2), (2, 3), (3, 2), (1, 1), (1, 3), (3, 1),
            (3, 3), (2, 0), (0, 2), (1, 0), (3, 0), (0, 1), (0, 3),
        ]
    ]
    for peer in peers:
        pl.semaphore_signal(barrier, inc=1, device_id={"mp": peer}, device_id_type=MESH)
    for load in loads[2:]:
        load.start()

    eye = iota((64, 128), 0) == iota((64, 128), 1)
    order = column_order((64, 128))
    for load in loads[:2]:
        load.wait()
    x = x_ref[...].astype(F32)
    gained = x * ngain_ref[...].astype(F32)
    gained = jnp.take_along_axis(gained, order, axis=1, mode="promise_in_bounds")
    xbuf[me, 0:64, :] = gained.astype(BF16)
    sums = jnp.broadcast_to(row_sums(x * x, eye), (8, 128))
    high = sums.astype(BF16).astype(F32)
    xbuf[me, 64:72, :] = jnp.where(iota((8, 128), 0) == 0, high, sums - high).astype(BF16)

    def copies(src, dst, send, recv):
        return [
            pltpu.make_async_remote_copy(
                src_ref=src(peer),
                dst_ref=dst.at[me],
                send_sem=send,
                recv_sem=recv,
                device_id={"mp": peer},
                device_id_type=MESH,
            )
            for peer in peers
        ]

    def wait_bytes(ref, sem):
        pltpu.make_async_copy(ref, ref, sem).wait()

    pl.semaphore_wait(barrier, n - 1)
    x_sends = copies(lambda peer: xbuf.at[me], xbuf, xs_sem, xr_sem.at[me // 2])
    for send in x_sends:
        send.start()

    def decode_gate_up(vals, mask, at):
        def body(i, carry):
            row = mask[pl.ds(i, 1), :].astype(F32) + F32(0.5)
            rows = vals[pl.ds(pl.multiple_of(i * 16, 16), 16), :]
            upper, lower = decode_rows(rows, row, 512)
            start = pl.multiple_of(i * 32, 32)
            wgu[pl.ds(start, 16), at : at + 512] = upper
            wgu[pl.ds(start + 16, 16), at : at + 512] = lower
            return carry

        lax.fori_loop(0, 64, body, 0)

    for load in loads[2:6]:
        load.wait()
    decode_gate_up(gv, gm, 0)
    decode_gate_up(uv, um, 512)
    for load in loads[6:]:
        load.wait()

    def decode_down(i, carry):
        for c in range(4):
            lanes = slice(c * 512, c * 512 + 512)
            row = dm[pl.ds(i, 1), lanes].astype(F32) + F32(0.5)
            rows = dv[pl.ds(pl.multiple_of(i * 16, 16), 16), lanes]
            upper, lower = decode_rows(rows, row, 512)
            start = pl.multiple_of(i * 32, 32)
            wd[pl.ds(start, 16), lanes] = upper
            wd[pl.ds(start + 16, 16), lanes] = lower
        return carry

    lax.fori_loop(0, 16, decode_down, 0)

    sums = jnp.zeros((1, 128), F32)
    for index, (dx, dy) in enumerate(
        [(0, 0), (0, 1), (1, 0), (3, 0), (1, 1), (3, 1), (2, 0), (2, 1)]
    ):
        pair = lax.rem(mx + dx, nx) * (ny // 2) + lax.rem(my // 2 + dy, ny // 2)
        wait_bytes(xbuf.at[pl.ds(0, 1 if index == 0 else 2)], xr_sem.at[pair])
        left, right = xbuf[2 * pair], xbuf[2 * pair + 1]
        block = jnp.concatenate([left[0:64], right[0:64]], axis=1)
        sides = left[64:72].astype(F32) + right[64:72].astype(F32)
        sums += sides[0:1] + sides[1:2]
        depth = pl.ds(pl.multiple_of(pair * 256, 256), 256)
        for c in range(2):
            lanes = slice(c * 512, c * 512 + 512)
            product = jnp.dot(block, wgu[depth, lanes], preferred_element_type=F32)
            if index == 0:
                acc[:, lanes] = product
            else:
                acc[:, lanes] += product

    scale = lax.rsqrt(row_column(sums, eye) / F32(n * 128) + F32(epsilon))
    gate = acc[:, 0:512] * scale
    up = acc[:, 512:1024] * scale
    hidden = jax.nn.silu(gate) * up
    hidden = jnp.concatenate(
        [
            jnp.take_along_axis(
                hidden[:, c * 128 : c * 128 + 128], order, axis=1, mode="promise_in_bounds"
            )
            for c in range(4)
        ],
        axis=1,
    ).astype(BF16)

    p_sends = copies(lambda peer: part.at[peer], rbuf, ps_sem, pr_sem)

    def down(first, second):
        rows = [wd[:, pl.ds(pl.multiple_of(to * 128, 128), 128)] for to in (first, second)]
        return jnp.dot(hidden, jnp.concatenate(rows, axis=1), preferred_element_type=F32)

    owners = peers + [me]
    product = down(*owners[0:2])
    for at in range(0, n, 2):
        later = down(*owners[at + 2 : at + 4]) if at + 2 < n else None
        product = product.astype(BF16)
        part[owners[at]] = product[:, 0:128]
        part[owners[at + 1]] = product[:, 128:256]
        for send in p_sends[at : at + 2]:
            send.start()
        product = later

    wait_bytes(rbuf.at[0 : n - 1], pr_sem)
    summed = part[me].astype(F32)
    for peer in peers:
        summed += rbuf[peer].astype(F32)
    out = (x_ref[...].astype(F32) + summed).astype(BF16)
    out = out.astype(F32)
    so_ref[...] = out
    sbuf[me] = row_sums(out * out, eye)
    s_sends = copies(lambda peer: sbuf.at[me], sbuf, ss_sem, sr_sem)
    for send in s_sends:
        send.start()
    wait_bytes(sbuf.at[0 : n - 1], sr_sem)
    scale = lax.rsqrt(row_column(jnp.sum(sbuf[:, 0, :], axis=0, keepdims=True), eye) / F32(n * 128) + F32(epsilon))
    fn_ref[...] = scale * fgain_ref[...].astype(F32)
    for ref, sem in [(xbuf, xs_sem), (part, ps_sem), (sbuf, ss_sem)]:
        wait_bytes(ref.at[0 : n - 1], sem)


def solution(mesh):
    n = mesh.shape["mp"]
    vmem = pl.BlockSpec(memory_space=pltpu.VMEM)
    hbm = pl.BlockSpec(memory_space=pl.ANY)

    def step(stream, ngain, gv, gm, uv, um, dv, dm, fgain):
        block = pltpu.VMEM(stream.shape, F32)
        dma = pltpu.SemaphoreType.DMA
        out, factor = pl.pallas_call(
            functools.partial(kernel, n, 4),
            out_shape=(block, block),
            in_specs=[hbm] * 9,
            out_specs=(vmem, vmem),
            scratch_shapes=[
                pltpu.VMEM(stream.shape, BF16),
                pltpu.VMEM((1, 128), BF16),
                pltpu.VMEM((1, 128), BF16),
                pltpu.VMEM(gv.shape, BF16),
                pltpu.VMEM(uv.shape, BF16),
                pltpu.VMEM(dv.shape, BF16),
                pltpu.VMEM(gm.shape, jnp.int32),
                pltpu.VMEM(um.shape, jnp.int32),
                pltpu.VMEM(dm.shape, jnp.int32),
                pltpu.VMEM((2048, 1024), BF16),
                pltpu.VMEM((512, 2048), BF16),
                pltpu.VMEM((64, 1024), F32),
                pltpu.VMEM((n, 72, 128), BF16),
                pltpu.VMEM((n, 64, 128), BF16),
                pltpu.VMEM((n, 64, 128), BF16),
                pltpu.VMEM((n, 1, 128), F32),
                dma((3,)),
                dma,
                dma((n // 2,)),
                dma,
                dma,
                dma,
                dma,
            ],
            compiler_params=pltpu.CompilerParams(collective_id=0, has_side_effects=True),
        )(stream, ngain.reshape(1, -1), fgain.reshape(1, -1), gv, gm, uv, um, dv, dm)
        return out.astype(BF16), (out * factor).astype(BF16)

    cols = P(None, "mp")
    return jax.shard_map(
        step,
        mesh=mesh,
        in_specs=(
            P("dp", "mp"),
            P("mp"),
            cols,
            cols,
            cols,
            cols,
            P("mp", None),
            P("mp", None),
            P("mp"),
        ),
        out_specs=(P("dp", "mp"), P("dp", "mp")),
        check_vma=False,
    )
```

time: 28.1 us -> 25.3 us (0.900)
  the two profiles are of different devices: /device:TPU:2 before, /device:TPU:8 now
where the time goes in v3:
time: 25.3 us; the launch traced here: 25.1 us
  Pallas kernels  23.8 us (94%)
  between operations  0.64 us (3%)
  other arithmetic  0.62 us (2%)
    pallas_call x1, Pallas kernels, step(): pl.pallas_call(functools.partial(kernel, n, 4), out_shape=(block, block),...  23.8 us
    convert_element_type x1, other arithmetic, step(): return (out.astype(BF16), (out * factor).astype(BF16))  0.62 us

profile of v3, /device:TPU:8, one launch (start us, length us, event | category | flops | bytes accessed | tf_op | source)
XLA Modules:
  0.0 25.1 jit_solution(16533024161810903109)
XLA Ops:
  0.6 23.8 %shard_map.104 = (f32[64,128]{1,0:T(8,128)S(1)}, f32[64,128]{1,0:T(8,128)S(1)}) custom-call(bf16[64,128]{1,0:T(8,128)(2,1)} %x_hbm.1, bf16[1,128]{1,0:T(2,128)(2,1)} %bitcast.2, bf16[1,128]{1,0:T(2,128)(2,1)} %bitcast.3, bf16[1024,512]{1,0:T(8,128)(2,1)} %gv_hbm.1, s32[64,512]{1,0:T(8,128)} %gm_hbm.1, bf16[1024,512]{1,0:T(8,128)(2,1)} %uv_hbm.1, ...), custom_call_target="tpu_custom_call" | custom-call | tf_op jit(solution)/shard_map/pallas_call | solution.py:283
  24.5 0.6 %multiply_convert_fusion = (bf16[64,128]{1,0:T(8,128)(2,1)}, bf16[64,128]{1,0:T(8,128)(2,1)}) fusion(f32[64,128]{1,0:T(8,128)S(1)} %get-tuple-element.4, f32[64,128]{1,0:T(8,128)S(1)} %get-tuple-element.5), kind=kLoop, calls=%fused_computation | loop fusion | flops 24576 | bytes 98304 | tf_op jit(solution)/shard_map/convert_element_type | solution.py:315

commit v4 on v3

--- a/solution.py
+++ b/solution.py
@@ -96,10 +96,13 @@
     wd,
     acc,
     xbuf,
+    qbuf,
     part,
     rbuf,
     sbuf,
     load_sem,
+    qs_sem,
+    qr_sem,
     xs_sem,
     xr_sem,
     ps_sem,
@@ -117,11 +120,11 @@
             (0, ngain_hbm, ngain_ref),
             (1, gm_hbm, gm),
             (1, gv_hbm, gv),
-            (1, um_hbm, um),
-            (1, uv_hbm, uv),
-            (2, dm_hbm, dm),
-            (2, dv_hbm, dv),
-            (2, fgain_hbm, fgain_ref),
+            (2, um_hbm, um),
+            (2, uv_hbm, uv),
+            (3, dm_hbm, dm),
+            (3, dv_hbm, dv),
+            (3, fgain_hbm, fgain_ref),
         ]
     ]
     for load in loads[:2]:
@@ -146,10 +149,8 @@
     x = x_ref[...].astype(F32)
     gained = x * ngain_ref[...].astype(F32)
     gained = jnp.take_along_axis(gained, order, axis=1, mode="promise_in_bounds")
-    xbuf[me, 0:64, :] = gained.astype(BF16)
-    sums = jnp.broadcast_to(row_sums(x * x, eye), (8, 128))
-    high = sums.astype(BF16).astype(F32)
-    xbuf[me, 64:72, :] = jnp.where(iota((8, 128), 0) == 0, high, sums - high).astype(BF16)
+    xbuf[me] = gained.astype(BF16)
+    qbuf[me] = row_sums(x * x, eye)
 
     def copies(src, dst, send, recv):
         return [
@@ -168,8 +169,9 @@
         pltpu.make_async_copy(ref, ref, sem).wait()
 
     pl.semaphore_wait(barrier, n - 1)
+    q_sends = copies(lambda peer: qbuf.at[me], qbuf, qs_sem, qr_sem)
     x_sends = copies(lambda peer: xbuf.at[me], xbuf, xs_sem, xr_sem.at[me // 2])
-    for send in x_sends:
+    for send in q_sends + x_sends:
         send.start()
 
     def decode_gate_up(vals, mask, at):
@@ -184,9 +186,11 @@
 
         lax.fori_loop(0, 64, body, 0)
 
-    for load in loads[2:6]:
+    for load in loads[2:4]:
         load.wait()
     decode_gate_up(gv, gm, 0)
+    for load in loads[4:6]:
+        load.wait()
     decode_gate_up(uv, um, 512)
     for load in loads[6:]:
         load.wait()
@@ -204,16 +208,16 @@
 
     lax.fori_loop(0, 16, decode_down, 0)
 
-    sums = jnp.zeros((1, 128), F32)
     for index, (dx, dy) in enumerate(
         [(0, 0), (0, 1), (1, 0), (3, 0), (1, 1), (3, 1), (2, 0), (2, 1)]
     ):
         pair = lax.rem(mx + dx, nx) * (ny // 2) + lax.rem(my // 2 + dy, ny // 2)
         wait_bytes(xbuf.at[pl.ds(0, 1 if index == 0 else 2)], xr_sem.at[pair])
-        left, right = xbuf[2 * pair], xbuf[2 * pair + 1]
-        block = jnp.concatenate([left[0:64], right[0:64]], axis=1)
-        sides = left[64:72].astype(F32) + right[64:72].astype(F32)
-        sums += sides[0:1] + sides[1:2]
+        block = jnp.concatenate([xbuf[2 * pair], xbuf[2 * pair + 1]], axis=1)
+        if index == 5:
+            wait_bytes(qbuf.at[0 : n - 1], qr_sem)
+            total = jnp.sum(qbuf[:, 0, :], axis=0, keepdims=True)
+            scale = lax.rsqrt(row_column(total, eye) / F32(n * 128) + F32(epsilon))
         depth = pl.ds(pl.multiple_of(pair * 256, 256), 256)
         for c in range(2):
             lanes = slice(c * 512, c * 512 + 512)
@@ -223,7 +227,6 @@
             else:
                 acc[:, lanes] += product
 
-    scale = lax.rsqrt(row_column(sums, eye) / F32(n * 128) + F32(epsilon))
     gate = acc[:, 0:512] * scale
     up = acc[:, 512:1024] * scale
     hidden = jax.nn.silu(gate) * up
@@ -268,7 +271,7 @@
     wait_bytes(sbuf.at[0 : n - 1], sr_sem)
     scale = lax.rsqrt(row_column(jnp.sum(sbuf[:, 0, :], axis=0, keepdims=True), eye) / F32(n * 128) + F32(epsilon))
     fn_ref[...] = scale * fgain_ref[...].astype(F32)
-    for ref, sem in [(xbuf, xs_sem), (part, ps_sem), (sbuf, ss_sem)]:
+    for ref, sem in [(qbuf, qs_sem), (xbuf, xs_sem), (part, ps_sem), (sbuf, ss_sem)]:
         wait_bytes(ref.at[0 : n - 1], sem)
 
 
@@ -298,11 +301,14 @@
                 pltpu.VMEM((2048, 1024), BF16),
                 pltpu.VMEM((512, 2048), BF16),
                 pltpu.VMEM((64, 1024), F32),
-                pltpu.VMEM((n, 72, 128), BF16),
+                pltpu.VMEM((n, 64, 128), BF16),
+                pltpu.VMEM((n, 1, 128), F32),
                 pltpu.VMEM((n, 64, 128), BF16),
                 pltpu.VMEM((n, 64, 128), BF16),
                 pltpu.VMEM((n, 1, 128), F32),
-                dma((3,)),
+                dma((4,)),
+                dma,
+                dma,
                 dma,
                 dma((n // 2,)),
                 dma,

time: 25.3 us -> 25.2 us (level)
  the two profiles are of different devices: /device:TPU:8 before, /device:TPU:2 now
where the time goes in v4:
time: 25.2 us; the launch traced here: 25 us
  Pallas kernels  23.7 us (94%)
  between operations  0.64 us (3%)
  other arithmetic  0.62 us (2%)
    pallas_call x1, Pallas kernels, step(): pl.pallas_call(functools.partial(kernel, n, 4), out_shape=(block, block),...  23.7 us
    convert_element_type x1, other arithmetic, step(): return (out.astype(BF16), (out * factor).astype(BF16))  0.62 us

profile of v4, /device:TPU:2, one launch (start us, length us, event | category | flops | bytes accessed | tf_op | source)
XLA Modules:
  0.0 25.0 jit_solution(9984730876595742098)
XLA Ops:
  0.6 23.7 %shard_map.104 = (f32[64,128]{1,0:T(8,128)S(1)}, f32[64,128]{1,0:T(8,128)S(1)}) custom-call(bf16[64,128]{1,0:T(8,128)(2,1)} %x_hbm.1, bf16[1,128]{1,0:T(2,128)(2,1)} %bitcast.2, bf16[1,128]{1,0:T(2,128)(2,1)} %bitcast.3, bf16[1024,512]{1,0:T(8,128)(2,1)} %gv_hbm.1, s32[64,512]{1,0:T(8,128)} %gm_hbm.1, bf16[1024,512]{1,0:T(8,128)(2,1)} %uv_hbm.1, ...), custom_call_target="tpu_custom_call" | custom-call | tf_op jit(solution)/shard_map/pallas_call | solution.py:286
  24.4 0.6 %multiply_convert_fusion = (bf16[64,128]{1,0:T(8,128)(2,1)}, bf16[64,128]{1,0:T(8,128)(2,1)}) fusion(f32[64,128]{1,0:T(8,128)S(1)} %get-tuple-element.4, f32[64,128]{1,0:T(8,128)S(1)} %get-tuple-element.5), kind=kLoop, calls=%fused_computation | loop fusion | flops 24576 | bytes 98304 | tf_op jit(solution)/shard_map/convert_element_type | solution.py:321

commit v5 on v4

--- a/solution.py
+++ b/solution.py
@@ -122,9 +122,9 @@
             (1, gv_hbm, gv),
             (2, um_hbm, um),
             (2, uv_hbm, uv),
-            (3, dm_hbm, dm),
-            (3, dv_hbm, dv),
-            (3, fgain_hbm, fgain_ref),
+            (2, dm_hbm, dm),
+            (2, dv_hbm, dv),
+            (2, fgain_hbm, fgain_ref),
         ]
     ]
     for load in loads[:2]:
@@ -189,11 +189,9 @@
     for load in loads[2:4]:
         load.wait()
     decode_gate_up(gv, gm, 0)
-    for load in loads[4:6]:
+    for load in loads[4:]:
         load.wait()
     decode_gate_up(uv, um, 512)
-    for load in loads[6:]:
-        load.wait()
 
     def decode_down(i, carry):
         for c in range(4):
@@ -219,26 +217,33 @@
             total = jnp.sum(qbuf[:, 0, :], axis=0, keepdims=True)
             scale = lax.rsqrt(row_column(total, eye) / F32(n * 128) + F32(epsilon))
         depth = pl.ds(pl.multiple_of(pair * 256, 256), 256)
-        for c in range(2):
-            lanes = slice(c * 512, c * 512 + 512)
-            product = jnp.dot(block, wgu[depth, lanes], preferred_element_type=F32)
-            if index == 0:
-                acc[:, lanes] = product
-            else:
-                acc[:, lanes] += product
-
-    gate = acc[:, 0:512] * scale
-    up = acc[:, 512:1024] * scale
-    hidden = jax.nn.silu(gate) * up
-    hidden = jnp.concatenate(
-        [
+        if index < 7:
+            for c in range(2):
+                lanes = slice(c * 512, c * 512 + 512)
+                product = jnp.dot(block, wgu[depth, lanes], preferred_element_type=F32)
+                if index == 0:
+                    acc[:, lanes] = product
+                else:
+                    acc[:, lanes] += product
+
+    hidden = []
+    for at in range(0, 512, 256):
+        gate, up = [
+            scale
+            * (
+                acc[:, lanes]
+                + jnp.dot(block, wgu[depth, lanes], preferred_element_type=F32)
+            )
+            for lanes in (slice(at, at + 256), slice(512 + at, 768 + at))
+        ]
+        product = jax.nn.silu(gate) * up
+        hidden += [
             jnp.take_along_axis(
-                hidden[:, c * 128 : c * 128 + 128], order, axis=1, mode="promise_in_bounds"
+                product[:, c : c + 128], order, axis=1, mode="promise_in_bounds"
             )
-            for c in range(4)
-        ],
-        axis=1,
-    ).astype(BF16)
+            for c in (0, 128)
+        ]
+    hidden = jnp.concatenate(hidden, axis=1).astype(BF16)
 
     p_sends = copies(lambda peer: part.at[peer], rbuf, ps_sem, pr_sem)
 
@@ -306,7 +311,7 @@
                 pltpu.VMEM((n, 64, 128), BF16),
                 pltpu.VMEM((n, 64, 128), BF16),
                 pltpu.VMEM((n, 1, 128), F32),
-                dma((4,)),
+                dma((3,)),
                 dma,
                 dma,
                 dma,

time: 25.2 us -> 25.2 us (level)
  no operation moved by 1% of the time
where the time goes in v5:
time: 25.2 us; the launch traced here: 25 us
  Pallas kernels  23.7 us (94%)
  between operations  0.64 us (3%)
  other arithmetic  0.62 us (2%)
    pallas_call x1, Pallas kernels, step(): pl.pallas_call(functools.partial(kernel, n, 4), out_shape=(block, block),...  23.7 us
    convert_element_type x1, other arithmetic, step(): return (out.astype(BF16), (out * factor).astype(BF16))  0.62 us

profile of v5, /device:TPU:2, one launch (start us, length us, event | category | flops | bytes accessed | tf_op | source)
XLA Modules:
  0.0 25.0 jit_solution(8263115016268912829)
XLA Ops:
  0.6 23.7 %shard_map.104 = (f32[64,128]{1,0:T(8,128)S(1)}, f32[64,128]{1,0:T(8,128)S(1)}) custom-call(bf16[64,128]{1,0:T(8,128)(2,1)} %x_hbm.1, bf16[1,128]{1,0:T(2,128)(2,1)} %bitcast.2, bf16[1,128]{1,0:T(2,128)(2,1)} %bitcast.3, bf16[1024,512]{1,0:T(8,128)(2,1)} %gv_hbm.1, s32[64,512]{1,0:T(8,128)} %gm_hbm.1, bf16[1024,512]{1,0:T(8,128)(2,1)} %uv_hbm.1, ...), custom_call_target="tpu_custom_call" | custom-call | tf_op jit(solution)/shard_map/pallas_call | solution.py:291
  24.4 0.6 %multiply_convert_fusion = (bf16[64,128]{1,0:T(8,128)(2,1)}, bf16[64,128]{1,0:T(8,128)(2,1)}) fusion(f32[64,128]{1,0:T(8,128)S(1)} %get-tuple-element.4, f32[64,128]{1,0:T(8,128)S(1)} %get-tuple-element.5), kind=kLoop, calls=%fused_computation | loop fusion | flops 24576 | bytes 98304 | tf_op jit(solution)/shard_map/convert_element_type | solution.py:326

commit v6 on v4

--- a/solution.py
+++ b/solution.py
@@ -152,7 +152,7 @@
     xbuf[me] = gained.astype(BF16)
     qbuf[me] = row_sums(x * x, eye)
 
-    def copies(src, dst, send, recv):
+    def copies(src, dst, send, recv, low=0, high=n - 1):
         return [
             pltpu.make_async_remote_copy(
                 src_ref=src(peer),
@@ -162,7 +162,7 @@
                 device_id={"mp": peer},
                 device_id_type=MESH,
             )
-            for peer in peers
+            for peer in peers[low:high]
         ]
 
     def wait_bytes(ref, sem):
@@ -240,7 +240,8 @@
         axis=1,
     ).astype(BF16)
 
-    p_sends = copies(lambda peer: part.at[peer], rbuf, ps_sem, pr_sem)
+    p_sends = copies(lambda peer: part.at[peer], rbuf, ps_sem, pr_sem.at[0], 0, 9)
+    p_sends += copies(lambda peer: part.at[peer], rbuf, ps_sem, pr_sem.at[1], 9)
 
     def down(first, second):
         rows = [wd[:, pl.ds(pl.multiple_of(to * 128, 128), 128)] for to in (first, second)]
@@ -257,11 +258,12 @@
             send.start()
         product = later
 
-    wait_bytes(rbuf.at[0 : n - 1], pr_sem)
-    summed = part[me].astype(F32)
-    for peer in peers:
-        summed += rbuf[peer].astype(F32)
-    out = (x_ref[...].astype(F32) + summed).astype(BF16)
+    summed = x_ref[...].astype(F32) + part[me].astype(F32)
+    for low, high in [(9, n - 1), (0, 9)]:
+        wait_bytes(rbuf.at[0 : high - low], pr_sem.at[low // 9])
+        for peer in peers[low:high]:
+            summed += rbuf[peer].astype(F32)
+    out = summed.astype(BF16)
     out = out.astype(F32)
     so_ref[...] = out
     sbuf[me] = row_sums(out * out, eye)
@@ -312,7 +314,7 @@
                 dma,
                 dma((n // 2,)),
                 dma,
-                dma,
+                dma((2,)),
                 dma,
                 dma,
             ],

time: 25.2 us -> 25.2 us (level)
  the two profiles are of different devices: /device:TPU:2 before, /device:TPU:8 now
where the time goes in v6:
time: 25.2 us; the launch traced here: 25 us
  Pallas kernels  23.8 us (94%)
  between operations  0.64 us (3%)
  other arithmetic  0.62 us (2%)
    pallas_call x1, Pallas kernels, step(): pl.pallas_call(functools.partial(kernel, n, 4), out_shape=(block, block),...  23.8 us
    convert_element_type x1, other arithmetic, step(): return (out.astype(BF16), (out * factor).astype(BF16))  0.62 us

profile of v6, /device:TPU:8, one launch (start us, length us, event | category | flops | bytes accessed | tf_op | source)
XLA Modules:
  0.0 25.0 jit_solution(8606343477556888554)
XLA Ops:
  0.6 23.8 %shard_map.104 = (f32[64,128]{1,0:T(8,128)S(1)}, f32[64,128]{1,0:T(8,128)S(1)}) custom-call(bf16[64,128]{1,0:T(8,128)(2,1)} %x_hbm.1, bf16[1,128]{1,0:T(2,128)(2,1)} %bitcast.2, bf16[1,128]{1,0:T(2,128)(2,1)} %bitcast.3, bf16[1024,512]{1,0:T(8,128)(2,1)} %gv_hbm.1, s32[64,512]{1,0:T(8,128)} %gm_hbm.1, bf16[1024,512]{1,0:T(8,128)(2,1)} %uv_hbm.1, ...), custom_call_target="tpu_custom_call" | custom-call | tf_op jit(solution)/shard_map/pallas_call | solution.py:288
  24.4 0.6 %multiply_convert_fusion = (bf16[64,128]{1,0:T(8,128)(2,1)}, bf16[64,128]{1,0:T(8,128)(2,1)}) fusion(f32[64,128]{1,0:T(8,128)S(1)} %get-tuple-element.4, f32[64,128]{1,0:T(8,128)S(1)} %get-tuple-element.5), kind=kLoop, calls=%fused_computation | loop fusion | flops 24576 | bytes 98304 | tf_op jit(solution)/shard_map/convert_element_type | solution.py:323
